TPU v7x, 128 devices: a whole 4x4x4 slice. The times are simulated.
128 devices in a mesh: front: 4 (over z_lo, core), grid: 32 (over z_hi, y, x).
Axes of the slice: x: 4, y: 4, z: 4 (z_hi: 2, z_lo: 2; z = z_hi * 2 + z_lo), core: 2. Of those that a mesh axis runs over, the one named last changes fastest.
Arguments:
- index_map: int32 [4, 8192], P('front'), may hold values from 0 to 16383, as said below
- lengths: int32 [4], P('front'), may hold values from 1 to 8192, 24576 in all
- update_front: float32 [4, 8192, 8192], P('front', 'grid'), may hold values from -0.0625 to 0.0625
- front_matrix: float32 [16384, 16384], P(('front', 'grid')), may hold values from -0.046875 to 0.046875
- random: float32 [16384, 256], P(('front', 'grid')), may hold values from -6 to 6
Outputs:
- parent_sample: float32 [16384, 256], P(('front', 'grid'))
Inputs may be any that keep to these rules, and one draw needn't show every extreme that they name: `index_map`: within one child the 8192 entries are distinct parent rows. `lengths`: rows of a child at or past its length are not live; the largest length equals 8192.
All inputs are finite; a program needn't handle non-finite values. No bound on the sum of `lengths` on one device may be relied on, other than what follows from the above.
Results may differ from a plain program's by a relative error of at most 0.0003.
Values sent between devices are 32-bit elements; how exact they have to be, the bound alone decides.
No kernel may reach another device: no remote copies, remote signals or barrier semaphores. Data moves between devices by JAX's collectives and lax.ppermute only.
A program may use at most 128 MiB of HBM per device.

v0:
```python
import jax
import jax.numpy as jnp
from jax import lax
from jax.sharding import PartitionSpec as P


def split_up(array, dim, length):
    shape = array.shape
    blocks = array.reshape(*shape[:dim], length, shape[dim] // length, *shape[dim + 1 :])
    return jnp.moveaxis(blocks, dim, 0)


def sum_at_owner(array, axis, dim):
    length = lax.axis_size(axis)
    blocks = lax.all_to_all(split_up(array, dim, length), axis, 0, 0, tiled=True)
    return jnp.sum(blocks, axis=0)


def shards(index_map, lengths, update_front, front_matrix, random):
    gathered_random = lax.all_gather(random, ("front", "grid"), axis=0, tiled=True)
    parent_part = jnp.dot(
        front_matrix,
        gathered_random,
        preferred_element_type=jnp.float32,
        precision=lax.Precision.HIGHEST,
    )
    index_rows = index_map[0]
    child_random = jnp.take(gathered_random, index_rows, axis=0)
    child_sample = jnp.dot(
        update_front[0],
        child_random,
        preferred_element_type=jnp.float32,
        precision=lax.Precision.HIGHEST,
    )
    local_rows = child_sample.shape[0]
    first_row = lax.axis_index("grid") * local_rows
    row_numbers = first_row + jnp.arange(local_rows, dtype=jnp.int32)
    live_rows = row_numbers < lengths[0]
    child_sample = jnp.where(live_rows[:, None], child_sample, jnp.float32(0.0))
    own_rows = parent_part.shape[0]
    group_sample = lax.all_gather(child_sample, "grid", axis=0, tiled=True)
    group_count = lax.axis_size("front")
    grid_count = lax.axis_size("grid")
    grid_place = lax.axis_index("grid")
    block_ids = jnp.arange(group_count, dtype=jnp.int32)[:, None] * grid_count + grid_place
    targets = (block_ids * own_rows + jnp.arange(own_rows, dtype=jnp.int32)[None, :]).reshape(-1)
    one_hot = (targets[:, None] == index_rows[None, :]).astype(jnp.float32)
    terms = jnp.dot(
        one_hot, group_sample, preferred_element_type=jnp.float32, precision=lax.Precision.HIGHEST
    )
    terms = terms.reshape(group_count, own_rows, terms.shape[1])
    added = sum_at_owner(terms, "front", 0)[0]
    return parent_part + added


def solution(mesh):
    placed = (
        P("front", None),
        P("front"),
        P("front", "grid", None),
        P(("front", "grid"), None),
        P(("front", "grid"), None),
    )
    return jax.shard_map(
        shards, mesh=mesh, in_specs=placed, out_specs=P(("front", "grid"), None), check_vma=False
    )
```

profile of v0, /device:TPU:1, one launch (start us, length us, event | category | flops | bytes accessed | tf_op | source)
XLA Modules:
  0.0 560.7 jit_solution(7659049847696991834)
XLA Ops:
  6.5 0.0 all-gather.3.cloned.1.call-start
  6.5 0.7 all-gather.3.cloned.1.call-update
  7.3 0.0 all-gather.5.cloned.1.call-start
  8.0 0.8 compare_and_fusion
  8.7 0.8 compare_select_fusion
  9.6 329.9 %all-gather.3.cloned.1.call-done = f32[16384,256]{1,0:T(8,128)} async-done(((f32[128,256]{1,0:T(8,128)}), f32[16384,256]{1,0:T(8,128)}) %all-gather.3.cloned.1.call-update) | async-done | bytes 16777232 | tf_op jit(solution)/shard_map/all_gather | solution.py:20
  339.5 37.3 %gather_fusion = f32[8192,256]{1,0:T(8,128)} fusion(f32[16384,256]{1,0:T(8,128)} %all-gather.3.cloned.1.call-done, s32[8192]{0:T(1024)S(1)} %broadcast_clamp_fusion), kind=kCustom, calls=%fused_computation | custom fusion | bytes 16809984 | tf_op jit(solution)/shard_map/jit(_take)/gather | solution.py:28
  376.8 0.0 copy-start
  376.8 21.5 %fusion.14 = f32[256,256]{0,1:T(8,128)} fusion(f32[1,256,8192]{2,1,0:T(8,128)} %param.7, f32[8192,256]{1,0:T(8,128)} %gather_fusion, pred[8192]{0:T(1024)(128)(4,1)S(1)} %compare_and_fusion, pred[256]{0:T(512)(128)(4,1)S(1)} %add_compare_fusion), kind=kOutput, calls=%fused_computation.11 | convolution fusion | flops 6444613632 | bytes 17047808 | tf_op jit(solution)/shard_map/dot_general | solution.py:29
  398.3 0.0 all-gather.5.cloned.1.call-update
  398.3 0.1 add_bitcast_fusion
  398.4 119.7 %all-gather.5.cloned.1.call-done = f32[8192,256]{0,1:T(8,128)} async-done(((f32[256,256]{0,1:T(8,128)}), f32[8192,256]{0,1:T(8,128)}) %all-gather.5.cloned.1.call-update) | async-done | bytes 8388624 | tf_op jit(solution)/shard_map/all_gather | solution.py:41
  518.1 0.0 copy-done
  518.1 10.6 %fusion = f32[512,256]{1,0:T(8,128)S(1)} fusion(f32[8192,256]{0,1:T(8,128)} %all-gather.5.cloned.1.call-done, s32[8192]{0:T(1024)S(1)} %bitcast.25, s32[512]{0:T(512)S(1)} %add_bitcast_fusion), kind=kOutput, calls=%fused_computation.1 | convolution fusion | flops 12889096192 | bytes 8947712 | tf_op jit(solution)/shard_map/dot_general | solution.py:48
  528.7 11.7 %all_to_all.5 = f32[4,1,128,256]{3,2,1,0:T(8,128)S(1)} all-to-all(f32[4,1,128,256]{3,2,1,0:T(8,128)S(1)} %bitcast.23), channel_id=1, replica_groups=mesh['front'=4,'grid'=32] {'front'}, dimensions={0} | all-to-all | bytes 1048576 | tf_op jit(solution)/shard_map/all_to_all | solution.py:15
  540.4 13.4 %convolution_add_fusion = f32[128,256]{1,0:T(8,128)} fusion(f32[128,256]{1,0:T(8,128)S(1)} %reduce_sum.9, f32[128,16384]{1,0:T(8,128)} %param.8, f32[16384,256]{1,0:T(8,128)} %all-gather.3.cloned.1.call-done), kind=kOutput, calls=%fused_computation.12 | convolution fusion | flops 6442483712 | bytes 25427968 | tf_op jit(solution)/shard_map/dot_general | solution.py:21
  (4 shorter events, 0.1 us)
Async XLA Ops:
  6.5 333.0 %all-gather.3.cloned.1.call-start = ((), (), s32[]{:S(2)}) async-start(), calls=%async_computation.1 | async-start | bytes 16908288 | tf_op jit(solution)/shard_map/all_gather | solution.py:20
  7.3 510.8 %all-gather.5.cloned.1.call-start = ((), (), s32[]{:S(2)}) async-start(), calls=%async_computation.2 | async-start | bytes 8650752 | tf_op jit(solution)/shard_map/all_gather | solution.py:41
  376.8 141.3 %copy-start = (s32[1,8192]{1,0:T(1,128)S(1)}, s32[1,8192]{1,0:T(1,128)}, u32[]{:S(2)}) copy-start(s32[1,8192]{1,0:T(1,128)} %param.5) | copy-start | bytes 98308
Sparse Core Ops, SparseCore 0:
  9.0 330.3 all-gather.2
  398.4 119.6 all-gather.4
where the time goes:
time: 561 us
  waiting for transfers between devices  450 us (80%)
  matrix products  45.5 us (8%)
  local copies, waits for them, and re-layouts  37.3 us (7%)
  between operations  14.1 us (3%)
  blocking collectives  11.7 us (2%)
    all_gather x1, waiting for transfers between devices, shards(): lax.all_gather(random, ('front', 'grid'), axis=0, tiled=True)  330 us
    all_gather x1, waiting for transfers between devices, shards(): group_sample = lax.all_gather(child_sample, 'grid', axis=0, tiled=True)  120 us
    gather x1, local copies, waits for them, and re-layouts, shards(): child_random = jnp.take(gathered_random, index_rows, axis=0)  37.3 us
    dot_general x1, matrix products, shards(): jnp.dot(update_front[0], child_random, preferred_element_type=jnp.float32...  21.5 us
    dot_general x1, matrix products, shards(): jnp.dot(front_matrix, gathered_random, preferred_element_type=jnp.float32...  13.4 us
    all_to_all x1, blocking collectives, sum_at_owner(): lax.all_to_all(split_up(array, dim, length), axis, 0, 0, tiled=True)  11.7 us
  transfers between devices with their start and end apart: 2, of which 2 were waited for; matrix products, arithmetic and copies ran while one was open for 0% of the time, Pallas kernels for 0%

commit v1 on v0

--- a/solution.py
+++ b/solution.py
@@ -38,7 +38,9 @@
     live_rows = row_numbers < lengths[0]
     child_sample = jnp.where(live_rows[:, None], child_sample, jnp.float32(0.0))
     own_rows = parent_part.shape[0]
-    group_sample = lax.all_gather(child_sample, "grid", axis=0, tiled=True)
+    group_sample = jnp.concatenate(
+        lax.all_to_all(jnp.stack([child_sample] * lax.axis_size("grid")), "grid", 0, 0), axis=0
+    )
     group_count = lax.axis_size("front")
     grid_count = lax.axis_size("grid")
     grid_place = lax.axis_index("grid")

time: 561 us -> 590 us (1.052); the launches traced: 561 us -> 581 us
  starting transfers between devices: 0.04 us -> 9.16 us
  waiting for transfers between devices: 450 us -> 459 us
    all_to_all x0 -> x1, waiting for transfers between devices: none -> 129 us  [shards(): lax.all_to_all(jnp.stack([child_sample] * lax.axis_size('grid')), 'grid',...]
    all_gather x1 -> x0, waiting for transfers between devices: 120 us -> none  [shards(): group_sample = lax.all_gather(child_sample, 'grid', axis=0, tiled=True)]
    all_to_all x0 -> x1, starting transfers between devices: none -> 9.16 us  [shards(): lax.all_to_all(jnp.stack([child_sample] * lax.axis_size('grid')), 'grid',...]
where the time goes in v1:
time: 590 us; the launch traced here: 581 us
  waiting for transfers between devices  459 us (78%)
  matrix products  44.7 us (8%)
  local copies, waits for them, and re-layouts  41.5 us (7%)
  between operations  14.1 us (2%)
  blocking collectives  10.7 us (2%)
  starting transfers between devices  9.16 us (2%)
    all_gather x1, waiting for transfers between devices, shards(): lax.all_gather(random, ('front', 'grid'), axis=0, tiled=True)  330 us
    all_to_all x1, waiting for transfers between devices, shards(): lax.all_to_all(jnp.stack([child_sample] * lax.axis_size('grid')), 'grid',...  129 us
    gather x1, local copies, waits for them, and re-layouts, shards(): child_random = jnp.take(gathered_random, index_rows, axis=0)  37.2 us
    dot_general x1, matrix products, shards(): jnp.dot(update_front[0], child_random, preferred_element_type=jnp.float32...  20.8 us
    dot_general x1, matrix products, shards(): jnp.dot(front_matrix, gathered_random, preferred_element_type=jnp.float32...  13.4 us
  transfers between devices with their start and end apart: 2, of which 2 were waited for; matrix products, arithmetic and copies ran while one was open for 0% of the time, Pallas kernels for 0%

profile of v1, /device:TPU:1, one launch (start us, length us, event | category | flops | bytes accessed | tf_op | source)
XLA Modules:
  0.0 581.1 jit_solution(851023029194631223)
XLA Ops:
  6.5 0.0 all-gather.2.cloned.1.call-start
  6.5 0.7 all-gather.2.cloned.1.call-update
  7.9 0.8 compare_and_fusion
  8.7 0.8 compare_select_fusion
  9.5 330.0 %all-gather.2.cloned.1.call-done = f32[16384,256]{1,0:T(8,128)} async-done(((f32[128,256]{1,0:T(8,128)}), f32[16384,256]{1,0:T(8,128)}) %all-gather.2.cloned.1.call-update) | async-done | bytes 16777232 | tf_op jit(solution)/shard_map/all_gather | solution.py:20
  339.5 37.2 %gather_fusion = f32[8192,256]{1,0:T(8,128)} fusion(f32[16384,256]{1,0:T(8,128)} %all-gather.2.cloned.1.call-done, s32[8192]{0:T(1024)S(1)} %broadcast_clamp_fusion), kind=kCustom, calls=%fused_computation | custom fusion | bytes 16809984 | tf_op jit(solution)/shard_map/jit(_take)/gather | solution.py:28
  376.7 20.8 %fusion.17 = f32[256,256]{0,1:T(8,128)S(1)} fusion(f32[1,256,8192]{2,1,0:T(8,128)} %param.7, f32[8192,256]{1,0:T(8,128)} %gather_fusion, pred[8192]{0:T(1024)(128)(4,1)S(1)} %compare_and_fusion, pred[256]{0:T(512)(128)(4,1)S(1)} %add_compare_fusion), kind=kOutput, calls=%fused_computation.12 | convolution fusion | flops 6444613632 | bytes 17047808 | tf_op jit(solution)/shard_map/dot_general | solution.py:29
  397.4 0.1 copy.8
  397.6 4.2 stack.2
  401.7 0.0 copy-start
  401.7 9.2 %all-to-all-start = ((f32[32,256,256]{2,1,0:T(8,128)}), f32[32,256,256]{2,1,0:T(8,128)}, u32[]{:S(2)}, u32[]{:S(2)}) async-start(f32[32,256,256]{2,1,0:T(8,128)} %stack.2), calls=%async_computation | async-start | bytes 16777216 | tf_op jit(solution)/shard_map/all_to_all | solution.py:42
  410.9 0.1 iota_add_fusion
  411.0 128.5 %all-to-all-done = f32[32,256,256]{2,1,0:T(8,128)} async-done(((f32[32,256,256]{2,1,0:T(8,128)}), f32[32,256,256]{2,1,0:T(8,128)}, u32[]{:S(2)}, u32[]{:S(2)}) %all-to-all-start) | async-done | bytes 8388640 | tf_op jit(solution)/shard_map/all_to_all | solution.py:42
  539.5 0.0 copy-done
  539.5 10.5 %fusion.9 = f32[4,1,128,256]{3,2,1,0:T(8,128)S(1)} fusion(f32[8192,256,1]{1,0,2:T(8,128)} %bitcast.7, s32[8192]{0:T(1024)S(1)} %bitcast.26, s32[4,128]{1,0:T(4,128)S(1)} %iota_add_fusion), kind=kOutput, calls=%fused_computation.10 | convolution fusion | flops 12889096192 | bytes 8947712 | tf_op jit(solution)/shard_map/dot_general | solution.py:50
  550.1 10.7 %all_to_all.10 = f32[4,1,128,256]{3,2,1,0:T(8,128)S(1)} all-to-all(f32[4,1,128,256]{3,2,1,0:T(8,128)S(1)} %fusion.9), channel_id=1, replica_groups=mesh['front'=4,'grid'=32] {'front'}, dimensions={0} | all-to-all | bytes 1048576 | tf_op jit(solution)/shard_map/all_to_all | solution.py:15
  560.8 13.4 %convolution_add_fusion = f32[128,256]{1,0:T(8,128)} fusion(f32[128,256]{1,0:T(8,128)S(1)} %reduce_sum.9, f32[128,16384]{1,0:T(8,128)} %param.8, f32[16384,256]{1,0:T(8,128)} %all-gather.2.cloned.1.call-done), kind=kOutput, calls=%fused_computation.13 | convolution fusion | flops 6442483712 | bytes 25427968 | tf_op jit(solution)/shard_map/dot_general | solution.py:21
  (4 shorter events, 0.1 us)
Async XLA Ops:
  6.5 333.0 %all-gather.2.cloned.1.call-start = ((), (), s32[]{:S(2)}) async-start(), calls=%async_computation.2 | async-start | bytes 16908288 | tf_op jit(solution)/shard_map/all_gather | solution.py:20
  401.7 137.8 %copy-start = (s32[1,8192]{1,0:T(1,128)S(1)}, s32[1,8192]{1,0:T(1,128)}, u32[]{:S(2)}) copy-start(s32[1,8192]{1,0:T(1,128)} %param.5) | copy-start | bytes 98308
  401.7 137.8 %all-to-all-start = ((f32[32,256,256]{2,1,0:T(8,128)}), f32[32,256,256]{2,1,0:T(8,128)}, u32[]{:S(2)}, u32[]{:S(2)}) async-start(f32[32,256,256]{2,1,0:T(8,128)} %stack.2), calls=%async_computation | async-start | bytes 16777216 | tf_op jit(solution)/shard_map/all_to_all | solution.py:42
Sparse Core Ops, SparseCore 0:
  9.0 330.3 all-gather.1
